TPU v7x, 256 devices: a whole 4x4x8 slice. The times are simulated.
256 devices in a mesh: view: 4 (over y_hi, core), tile: 64 (over z, y_lo, x).
Axes of the slice: x: 4, y: 4 (y_hi: 2, y_lo: 2; y = y_hi * 2 + y_lo), z: 8, core: 2. Of those that a mesh axis runs over, the one named last changes fastest.
Arguments:
- data: bfloat16 [8, 2560, 64, 128], P('view', 'tile'), may hold values from 0.1 to 5, as said below
- estimate: float32 [2560, 64, 128], P('tile'), may hold values from 0.5 to 2
- psf_taps: float32 [8, 3, 31], P('view'), may hold values from 0.03 to 1.6, as said below
Outputs:
- restored: float32 [2560, 64, 128], P('tile')
Inputs may be any that keep to these rules, and one draw needn't show every extreme that they name: `data`: positive recorded intensities. `psf_taps`: positive taps.
All inputs are finite; a program needn't handle non-finite values.
Results may differ from a plain program's by a relative error of at most 0.0003.
Values may be sent and summed in bfloat16 or wider, within the bound.
A program may use at most 64 MiB of HBM per device.

v0:
```python
import jax
import jax.numpy as jnp
from jax import lax
from jax.experimental import pallas as pl
from jax.experimental.pallas import tpu as pltpu
from jax.sharding import PartitionSpec as P

ITERS = 3
GROUP = 4
F32 = jnp.float32
BF16 = jnp.bfloat16
MESH = pl.DeviceIdType.MESH


def band(taps, n_rows, n_cols, shift):
    offset = jnp.arange(n_cols)[None, :] - jnp.arange(n_rows)[:, None] + shift
    hit = offset[:, :, None] == jnp.arange(taps.shape[-1])[None, None, :]
    return jnp.sum(jnp.where(hit[None], taps[:, None, None, :], 0.0), axis=3)


def split(w):
    hi = w.astype(BF16)
    return hi, (w - hi.astype(F32)).astype(BF16)


def split_weights(w):
    hi = lax.reduce_precision(w, 8, 7)
    return hi.astype(BF16), (w - hi).astype(BF16)


def dot(a, b):
    return jnp.dot(a, b, preferred_element_type=F32)


def make_weights(taps, ny, nz, rows, ext, mid, ext_pad, mid_pad):
    half = taps.shape[2] // 2
    flipped = taps[:, :, ::-1]
    cat = jnp.concatenate

    def along_x(t, n_out, n_in, out_pad, in_pad):
        w = band(t, n_out, n_in, 0)
        w = jnp.pad(w, ((0, 0), (0, out_pad - n_out), (0, in_pad - n_in)))
        return cat(split_weights(w), axis=2)

    xf = along_x(taps[:, 0], mid, ext, mid_pad, ext_pad)
    xa = along_x(flipped[:, 0], rows, mid, rows, mid_pad)
    yf = cat(split_weights(band(taps[:, 1], ny, ny, half)), axis=2)
    hi, lo = split_weights(band(flipped[:, 1], ny, ny, half))
    ya = cat([hi, lo, hi], axis=2)
    hi, lo = split_weights(band(flipped[:, 2], nz, nz, half))
    zf = cat([cat([hi[0], hi[1]], axis=1), cat([lo[0], lo[1]], axis=1)], axis=0)
    hi, lo = split_weights(band(taps[:, 2], nz, nz, half))
    za = cat([cat([hi[0], lo[0]], axis=1), cat([hi[1], lo[1]], axis=1)], axis=0)
    return xf, yf, zf, xa, ya, za


def shards(data, estimate, psf_taps):
    views, rows, ny, nz = data.shape
    half = psf_taps.shape[2] // 2
    total_views = views * lax.axis_size("view")
    tiles = lax.axis_size("tile")
    wide = 2 * half
    ext = rows + 2 * wide
    mid = rows + 2 * half
    ext_pad = -(-ext // 16) * 16
    mid_pad = -(-mid // 16) * 16
    ch = rows // 4
    weights = make_weights(psf_taps, ny, nz, rows, ext, mid, ext_pad, mid_pad)

    def kernel(data_ref, est_ref, xf, yf, zf, xa, ya, za, out_ref,
               extb, zb, xb, rb, ab, yb, dx, em, ps, pr, po, hs, hr, fin,
               lsem, dsem_s, dsem_r, hsem_s, hsem_r, fsem_s, fsem_r,
               psem_s, psem_r, ysem_s, ysem_r, osem_s, osem_r):
        t = lax.axis_index("tile")
        v = lax.axis_index("view")
        c = lax.rem(v, 2)
        other = (v - c) + (1 - c)
        across = lax.rem(v + 2, 4)
        left = lax.rem(t + tiles - 1, tiles)
        right = lax.rem(t + 1, tiles)
        has_left = t > 0
        has_right = t < tiles - 1

        cp_est = pltpu.make_async_copy(est_ref, em, lsem.at[0])
        cp_dat = pltpu.make_async_copy(data_ref, dx.at[:, pl.ds(half, rows)], lsem.at[1])
        cp_est.start()
        cp_dat.start()

        barrier = pltpu.get_barrier_semaphore()
        for who in ((t, other), (t, across), (left, v), (right, v)):
            pl.semaphore_signal(barrier, inc=1, device_id=(who[1], who[0]), device_id_type=MESH)
        pl.semaphore_wait(barrier, 4)

        def remote(src, dst, s_sem, r_sem, tile, view):
            return pltpu.make_async_remote_copy(
                src_ref=src, dst_ref=dst, send_sem=s_sem, recv_sem=r_sem,
                device_id=(view, tile), device_id_type=MESH)

        inner = ch + ch * c
        outer = 3 * ch * c
        c_tile = jnp.where(c == 0, left, right)
        c_send = ((c == 0) & has_left) | ((c == 1) & has_right)
        c_recv = ((c == 0) & has_right) | ((c == 1) & has_left)

        def own(k, row):
            return extb.at[k, pl.ds(wide + row, ch)]

        def piece(k, which):
            if which == 0:
                src, at, tile, give, take = inner, ext - wide + ch + ch * c, left, has_left, has_right
            elif which == 1:
                src, at, tile, give, take = inner, ch * c, right, has_right, has_left
            else:
                src, at, tile, give, take = outer, (ext - wide) - (ext - wide - 2 * ch) * c, c_tile, c_send, c_recv
            return src, at, tile, give, take

        def halo(k, which):
            src, at, tile, give, take = piece(k, which)
            return remote(own(k, src), extb.at[k, pl.ds(at, ch)],
                          hsem_s.at[k, which], hsem_r.at[k, which], tile, v)

        def forward(k, which):
            src, at, tile, give, take = piece(k, which)
            return remote(extb.at[k, pl.ds(at, ch)], extb.at[k, pl.ds(at, ch)],
                          fsem_s.at[k, which], fsem_r.at[k, which], t, other)

        def forwarded(k, which):
            d = 1 - c
            if which == 0:
                at, take = ext - wide + ch + ch * d, has_right
            elif which == 1:
                at, take = ch * d, has_left
            else:
                at = (ext - wide) - (ext - wide - 2 * ch) * d
                take = ((d == 0) & has_right) | ((d == 1) & has_left)
            return remote(extb.at[k, pl.ds(at, ch)], extb.at[k, pl.ds(at, ch)],
                          fsem_s.at[k, which], fsem_r.at[k, which], t, other), take

        def start_halo(k, which):
            give = piece(k, which)[3]

            @pl.when(give)
            def _():
                halo(k, which).start()

        def finish_halo(k):
            for which in (0, 1, 2):
                take = piece(k, which)[4]

                @pl.when(take)
                def _():
                    halo(k, which).wait_recv()
                    forward(k, which).start()
            for which in (0, 1, 2):
                cp, take = forwarded(k, which)

                @pl.when(take)
                def _():
                    cp.wait_recv()

        def drain_halo(k):
            for which in (0, 1, 2):
                src, at, tile, give, take = piece(k, which)

                @pl.when(give)
                def _():
                    halo(k, which).wait_send()

                @pl.when(take)
                def _():
                    forward(k, which).wait_send()

        to_right = remote(data_ref.at[:, pl.ds(rows - half, half)], dx.at[:, pl.ds(0, half)],
                          dsem_s.at[0], dsem_r.at[0], right, v)
        to_left = remote(data_ref.at[:, pl.ds(0, half)], dx.at[:, pl.ds(half + rows, half)],
                         dsem_s.at[1], dsem_r.at[1], left, v)

        cp_est.wait()
        extb[0, pl.ds(wide, rows)] = em[...].astype(BF16)
        for which in (0, 1, 2):
            start_halo(0, which)

        @pl.when(has_right)
        def _():
            to_right.start()

        @pl.when(has_left)
        def _():
            to_left.start()

        @pl.when(t == 0)
        def _():
            for k in range(ITERS):
                extb[k, pl.ds(0, wide)] = jnp.zeros((wide, ny, nz), BF16)
            for i in range(views):
                dx[i, pl.ds(0, half)] = jnp.zeros((half, ny, nz), BF16)

        @pl.when(t == tiles - 1)
        def _():
            for k in range(ITERS):
                extb[k, pl.ds(ext - wide, wide)] = jnp.zeros((wide, ny, nz), BF16)
            for i in range(views):
                dx[i, pl.ds(half + rows, half)] = jnp.zeros((half, ny, nz), BF16)

        for i in range(views):
            zb[i, pl.ds(ext * ny, (ext_pad - ext) * ny), :] = jnp.zeros(((ext_pad - ext) * ny, nz), F32)
            rb[i, pl.ds(mid * ny, (mid_pad - mid) * ny), :] = jnp.zeros(((mid_pad - mid) * ny, nz), F32)

        def blur_z(k):
            step = ext // 10

            def body(j, _):
                lhs = extb[k, pl.ds(j * step, step)].reshape(step * ny, nz)
                o = dot(jnp.concatenate([lhs, lhs], axis=1), zf[...])
                at = pl.multiple_of(j * step * ny, step * ny)
                for i in range(views):
                    zb[i, pl.ds(at, step * ny), :] = o[:, i * nz:(i + 1) * nz]
                return 0
            lax.fori_loop(0, 10, body, 0)

        def conv_x(src, dst, w, n_in, n_out):
            def body(j, _):
                outs = []
                for u in range(GROUP):
                    y = 2 * (GROUP * j + u)
                    for i in range(views):
                        a = src[i, pl.ds(y, n_in, stride=ny), :]
                        b = src[i, pl.ds(y + 1, n_in, stride=ny), :]
                        r = jnp.concatenate([a, b], axis=1).astype(BF16)
                        outs.append((y, i, dot(w[i], jnp.concatenate([r, r], axis=0))))
                for y, i, o in outs:
                    dst[i, pl.ds(y, n_out, stride=ny), :] = o[:, :nz]
                    dst[i, pl.ds(y + 1, n_out, stride=ny), :] = o[:, nz:]
                return 0
            lax.fori_loop(0, ny // (2 * GROUP), body, 0)

        def ratios():
            def body(j, _):
                outs = []
                for u in range(5):
                    at = pl.multiple_of((5 * j + u) * 2 * ny, 2 * ny)
                    for i in range(views):
                        r = jnp.concatenate([xb[i, pl.ds(at, ny), :], xb[i, pl.ds(at + ny, ny), :]], axis=1).astype(BF16)
                        o = dot(yf[i], jnp.concatenate([r, r], axis=0))
                        row = 2 * (5 * j + u)
                        outs.append((at, i, dx[i, row].astype(F32) / o[:, :nz],
                                     dx[i, row + 1].astype(F32) / o[:, nz:]))
                for at, i, p, q in outs:
                    rb[i, pl.ds(at, ny), :] = p
                    rb[i, pl.ds(at + ny, ny), :] = q
                return 0
            lax.fori_loop(0, mid // 10, body, 0)

        def adjoint_rows(row):
            for j in range(ch // 2):
                at = pl.multiple_of((row + 2 * j) * ny, 2 * ny)
                to = j * 2 * ny
                for i in range(views):
                    r = jnp.concatenate([ab[i, pl.ds(at, ny), :], ab[i, pl.ds(at + ny, ny), :]], axis=1)
                    hi, lo = split(r)
                    o = dot(ya[i], jnp.concatenate([hi, hi, lo], axis=0))
                    yb[pl.ds(to, ny), i * nz:(i + 1) * nz] = o[:, :nz]
                    yb[pl.ds(to + ny, ny), i * nz:(i + 1) * nz] = o[:, nz:]
            hi, lo = split(yb[...])
            o = dot(hi, za[...])
            o = o[:, :nz] + o[:, nz:] + dot(lo, za[:, :nz])
            return o.reshape(ch, ny, nz)

        def partner(k, p):
            return remote(ps.at[k, p], pr.at[k, p], psem_s.at[k, p], psem_r.at[k, p], t, other)

        def over(k, p):
            return remote(hs.at[k, p], hr.at[k, p], ysem_s.at[k, p], ysem_r.at[k, p], t, across)

        def share(k, p):
            row = (inner, outer)[p]
            return remote(own(k + 1, row), own(k + 1, row), osem_s.at[k, p], osem_r.at[k, p], t, other)

        def shared(k, p):
            row = (ch + ch * (1 - c), 3 * ch * (1 - c))[p]
            return remote(own(k + 1, row), own(k + 1, row), osem_s.at[k, p], osem_r.at[k, p], t, other)

        finish_halo(0)
        cp_dat.wait()

        def iteration(k, _):
            blur_z(k)
            conv_x(zb, xb, xf, ext_pad, mid_pad)

            @pl.when((k == 0) & has_left)
            def _():
                to_right.wait_recv()

            @pl.when((k == 0) & has_right)
            def _():
                to_left.wait_recv()

            ratios()
            conv_x(rb, ab, xa, mid_pad, rows)
            theirs = (ch + ch * (1 - c), 3 * ch * (1 - c))
            ours = (inner, outer)
            for p in (0, 1):
                ps[k, p] = adjoint_rows(theirs[p])
                partner(k, p).start()
                po[p] = adjoint_rows(ours[p])
                partner(k, p).wait_recv()
                hs[k, p] = po[p] + pr[k, p]
                over(k, p).start()
            for p in (0, 1):
                over(k, p).wait_recv()
                rows_here = pl.ds(ours[p], ch)
                em[rows_here] = em[rows_here] * (hs[k, p] + hr[k, p]) / total_views

                @pl.when(k < ITERS - 1)
                def _():
                    extb[k + 1, pl.ds(wide + ours[p], ch)] = em[rows_here].astype(BF16)
                    for which in ((0, 1), (2,))[p]:
                        start_halo(k + 1, which)
                    share(k, p).start()

            @pl.when(k < ITERS - 1)
            def _():
                finish_halo(k + 1)
                for p in (0, 1):
                    shared(k, p).wait_recv()
            return 0

        lax.fori_loop(0, ITERS, iteration, 0)

        ends = []
        for p in (0, 1):
            row = (inner, outer)[p]
            fin[p] = em[pl.ds(row, ch)]
            here = pltpu.make_async_copy(fin.at[p], out_ref.at[pl.ds(row, ch)], lsem.at[2 + p])
            there = remote(fin.at[p], out_ref.at[pl.ds(row, ch)],
                           osem_s.at[ITERS - 1, p], osem_r.at[ITERS - 1, p], t, other)
            here.start()
            there.start()
            ends += [here, there]
        for cp in ends:
            cp.wait()

        @pl.when(has_right)
        def _():
            to_right.wait_send()

        @pl.when(has_left)
        def _():
            to_left.wait_send()

        for k in range(ITERS):
            drain_halo(k)
            for p in (0, 1):
                partner(k, p).wait_send()
                over(k, p).wait_send()
                if k < ITERS - 1:
                    share(k, p).wait_send()

    vmem = pltpu.VMEM
    dma = pltpu.SemaphoreType.DMA
    block = (ch, ny, nz)
    return pl.pallas_call(
        kernel,
        out_shape=jax.ShapeDtypeStruct(estimate.shape, F32),
        in_specs=[pl.BlockSpec(memory_space=pl.ANY)] * 2 + [pl.BlockSpec(memory_space=vmem)] * 6,
        out_specs=pl.BlockSpec(memory_space=pl.ANY),
        scratch_shapes=[
            vmem((ITERS, ext, ny, nz), BF16),
            vmem((views, ext_pad * ny, nz), F32),
            vmem((views, mid_pad * ny, nz), F32),
            vmem((views, mid_pad * ny, nz), F32),
            vmem((views, rows * ny, nz), F32),
            vmem((ch * ny, views * nz), F32),
            vmem((views, mid, ny, nz), BF16),
            vmem((rows, ny, nz), F32),
            vmem((ITERS, 2) + block, F32),
            vmem((ITERS, 2) + block, F32),
            vmem((2,) + block, F32),
            vmem((ITERS, 2) + block, F32),
            vmem((ITERS, 2) + block, F32),
            vmem((2,) + block, F32),
            dma((4,)), dma((2,)), dma((2,)),
            dma((ITERS, 3)), dma((ITERS, 3)), dma((ITERS, 3)), dma((ITERS, 3)),
            dma((ITERS, 2)), dma((ITERS, 2)), dma((ITERS, 2)), dma((ITERS, 2)),
            dma((ITERS, 2)), dma((ITERS, 2)),
        ],
        compiler_params=pltpu.CompilerParams(
            collective_id=0, has_side_effects=True, vmem_limit_bytes=60 * 1024 * 1024),
    )(data, estimate, *weights)


def solution(mesh):
    placed = (P("view", "tile", None, None), P("tile", None, None), P("view", None, None))
    return jax.shard_map(
        shards, mesh=mesh, in_specs=placed, out_specs=P("tile", None, None), check_vma=False
    )
```

profile of v0, /device:TPU:225, one launch (start us, length us, event | category | flops | bytes accessed | tf_op | source)
XLA Modules:
  0.0 162.8 jit_solution(9739439573494042554)
XLA Ops:
  0.0 0.7 fusion.6
  0.7 0.1 slice.53
  0.8 0.1 slice.48
  0.9 0.1 slice.54
  1.0 0.1 copy.4
  1.1 0.1 iota_compare_fusion.3
  1.2 0.2 select_reduce_fusion.5
  1.5 0.7 pad_maximum_fusion.2.xa
  2.2 0.1 iota_compare_fusion.2
  2.3 0.5 select_reduce_fusion.3
  2.9 0.7 pad_maximum_fusion.3.yf
  3.6 0.7 pad_maximum_fusion.1.ya
  4.3 0.2 iota_compare_fusion.1
  4.5 2.3 %select_reduce_fusion.2 = f32[2,70,100]{2,0,1:T(2,128)S(1)} fusion(pred[70,100,31]{1,2,0:T(8,128)(4,1)S(1)} %iota_compare_fusion.1, f32[2,31]{0,1:T(8,128)S(1)} %copy.4), kind=kLoop, calls=%fused_computation.2 | loop fusion | flops 854000 | bytes 273248 | tf_op jit(solution)/shard_map/reduce_sum | solution.py:18
  6.8 0.7 pad_maximum_fusion.xf
  7.5 0.3 iota_compare_fusion
  7.8 1.0 select_reduce_fusion
  9.0 0.7 maximum_maximum_fusion.1.za
  9.6 0.7 maximum_maximum_fusion.zf
  10.3 150.0 %shard_map.37 = f32[40,64,128]{2,1,0:T(8,128)} custom-call(bf16[2,40,64,128]{3,2,1,0:T(8,128)(2,1)} %data_ref.1, f32[40,64,128]{2,1,0:T(8,128)} %est_ref.1, bf16[2,80,224]{2,1,0:T(8,128)(2,1)} %pad_maximum_fusion.xf, bf16[2,64,128]{2,1,0:T(8,128)(2,1)} %pad_maximum_fusion.3.yf, bf16[256,256]{1,0:T(8,128)(2,1)} %maximum_maximum_fusion.zf, ...), custom_call_target="tpu_custom_call" | custom-call | tf_op jit(solution)/shard_map/pallas_call | solution.py:362
  160.3 2.5 %copy.7 = f32[40,64,128]{2,1,0:T(8,128)} copy(f32[40,64,128]{2,1,0:T(8,128)} %shard_map.37) | data formatting | bytes 2621440
  (13 shorter events, 0.2 us)
where the time goes:
time: 163 us
  Pallas kernels  150 us (92%)
  other arithmetic  9.06 us (6%)
  local copies, waits for them, and re-layouts  3.65 us (2%)
    pallas_call x1, Pallas kernels, shards(): pl.pallas_call(kernel, out_shape=jax.ShapeDtypeStruct(estimate.shape, F32...  150 us
    reduce_sum x4, other arithmetic, band(): return jnp.sum(jnp.where(hit[None], taps[:, None, None, :], 0.0), axis=3)  4.07 us

commit v1 on v0

--- a/solution.py
+++ b/solution.py
@@ -7,6 +7,7 @@
 
 ITERS = 3
 GROUP = 4
+ST = 65
 F32 = jnp.float32
 BF16 = jnp.bfloat16
 MESH = pl.DeviceIdType.MESH
@@ -203,8 +204,8 @@
                 dx[i, pl.ds(half + rows, half)] = jnp.zeros((half, ny, nz), BF16)
 
         for i in range(views):
-            zb[i, pl.ds(ext * ny, (ext_pad - ext) * ny), :] = jnp.zeros(((ext_pad - ext) * ny, nz), F32)
-            rb[i, pl.ds(mid * ny, (mid_pad - mid) * ny), :] = jnp.zeros(((mid_pad - mid) * ny, nz), F32)
+            zb[i, pl.ds(ext * ST, (ext_pad - ext) * ST), :] = jnp.zeros(((ext_pad - ext) * ST, nz), F32)
+            rb[i, pl.ds(mid * ST, (mid_pad - mid) * ST), :] = jnp.zeros(((mid_pad - mid) * ST, nz), F32)
 
         def blur_z(k):
             step = ext // 10
@@ -212,9 +213,9 @@
             def body(j, _):
                 lhs = extb[k, pl.ds(j * step, step)].reshape(step * ny, nz)
                 o = dot(jnp.concatenate([lhs, lhs], axis=1), zf[...])
-                at = pl.multiple_of(j * step * ny, step * ny)
-                for i in range(views):
-                    zb[i, pl.ds(at, step * ny), :] = o[:, i * nz:(i + 1) * nz]
+                for q in range(step):
+                    for i in range(views):
+                        zb[i, pl.ds((j * step + q) * ST, ny), :] = o[q * ny:(q + 1) * ny, i * nz:(i + 1) * nz]
                 return 0
             lax.fori_loop(0, 10, body, 0)
 
@@ -224,13 +225,13 @@
                 for u in range(GROUP):
                     y = 2 * (GROUP * j + u)
                     for i in range(views):
-                        a = src[i, pl.ds(y, n_in, stride=ny), :]
-                        b = src[i, pl.ds(y + 1, n_in, stride=ny), :]
+                        a = src[i, pl.ds(y, n_in, stride=ST), :]
+                        b = src[i, pl.ds(y + 1, n_in, stride=ST), :]
                         r = jnp.concatenate([a, b], axis=1).astype(BF16)
                         outs.append((y, i, dot(w[i], jnp.concatenate([r, r], axis=0))))
                 for y, i, o in outs:
-                    dst[i, pl.ds(y, n_out, stride=ny), :] = o[:, :nz]
-                    dst[i, pl.ds(y + 1, n_out, stride=ny), :] = o[:, nz:]
+                    dst[i, pl.ds(y, n_out, stride=ST), :] = o[:, :nz]
+                    dst[i, pl.ds(y + 1, n_out, stride=ST), :] = o[:, nz:]
                 return 0
             lax.fori_loop(0, ny // (2 * GROUP), body, 0)
 
@@ -238,25 +239,25 @@
             def body(j, _):
                 outs = []
                 for u in range(5):
-                    at = pl.multiple_of((5 * j + u) * 2 * ny, 2 * ny)
+                    at = (5 * j + u) * 2 * ST
                     for i in range(views):
-                        r = jnp.concatenate([xb[i, pl.ds(at, ny), :], xb[i, pl.ds(at + ny, ny), :]], axis=1).astype(BF16)
+                        r = jnp.concatenate([xb[i, pl.ds(at, ny), :], xb[i, pl.ds(at + ST, ny), :]], axis=1).astype(BF16)
                         o = dot(yf[i], jnp.concatenate([r, r], axis=0))
                         row = 2 * (5 * j + u)
                         outs.append((at, i, dx[i, row].astype(F32) / o[:, :nz],
                                      dx[i, row + 1].astype(F32) / o[:, nz:]))
                 for at, i, p, q in outs:
                     rb[i, pl.ds(at, ny), :] = p
-                    rb[i, pl.ds(at + ny, ny), :] = q
+                    rb[i, pl.ds(at + ST, ny), :] = q
                 return 0
             lax.fori_loop(0, mid // 10, body, 0)
 
         def adjoint_rows(row):
             for j in range(ch // 2):
-                at = pl.multiple_of((row + 2 * j) * ny, 2 * ny)
+                at = (row + 2 * j) * ST
                 to = j * 2 * ny
                 for i in range(views):
-                    r = jnp.concatenate([ab[i, pl.ds(at, ny), :], ab[i, pl.ds(at + ny, ny), :]], axis=1)
+                    r = jnp.concatenate([ab[i, pl.ds(at, ny), :], ab[i, pl.ds(at + ST, ny), :]], axis=1)
                     hi, lo = split(r)
                     o = dot(ya[i], jnp.concatenate([hi, hi, lo], axis=0))
                     yb[pl.ds(to, ny), i * nz:(i + 1) * nz] = o[:, :nz]
@@ -366,10 +367,10 @@
         out_specs=pl.BlockSpec(memory_space=pl.ANY),
         scratch_shapes=[
             vmem((ITERS, ext, ny, nz), BF16),
-            vmem((views, ext_pad * ny, nz), F32),
-            vmem((views, mid_pad * ny, nz), F32),
-            vmem((views, mid_pad * ny, nz), F32),
-            vmem((views, rows * ny, nz), F32),
+            vmem((views, ext_pad * ST, nz), F32),
+            vmem((views, mid_pad * ST, nz), F32),
+            vmem((views, mid_pad * ST, nz), F32),
+            vmem((views, rows * ST, nz), F32),
             vmem((ch * ny, views * nz), F32),
             vmem((views, mid, ny, nz), BF16),
             vmem((rows, ny, nz), F32),

time: 163 us -> 138 us (0.85)
  Pallas kernels: 150 us -> 125 us
    pallas_call x1, Pallas kernels: 150 us -> 125 us  [shards(): pl.pallas_call(kernel, out_shape=jax.ShapeDtypeStruct(estimate.shape, F32...]
where the time goes in v1:
time: 138 us
  Pallas kernels  125 us (91%)
  other arithmetic  9.06 us (7%)
  local copies, waits for them, and re-layouts  3.65 us (3%)
    pallas_call x1, Pallas kernels, shards(): pl.pallas_call(kernel, out_shape=jax.ShapeDtypeStruct(estimate.shape, F32...  125 us
    reduce_sum x4, other arithmetic, band(): return jnp.sum(jnp.where(hit[None], taps[:, None, None, :], 0.0), axis=3)  4.07 us

profile of v1, /device:TPU:225, one launch (start us, length us, event | category | flops | bytes accessed | tf_op | source)
XLA Modules:
  0.0 137.7 jit_solution(16735826923412509882)
XLA Ops:
  0.0 0.7 fusion.6
  0.7 0.1 slice.53
  0.8 0.1 slice.48
  0.9 0.1 slice.54
  1.0 0.1 copy.4
  1.1 0.1 iota_compare_fusion.3
  1.2 0.2 select_reduce_fusion.5
  1.5 0.7 pad_maximum_fusion.2.xa
  2.2 0.1 iota_compare_fusion.2
  2.3 0.5 select_reduce_fusion.3
  2.9 0.7 pad_maximum_fusion.3.yf
  3.6 0.7 pad_maximum_fusion.1.ya
  4.3 0.2 iota_compare_fusion.1
  4.5 2.3 %select_reduce_fusion.2 = f32[2,70,100]{2,0,1:T(2,128)S(1)} fusion(pred[70,100,31]{1,2,0:T(8,128)(4,1)S(1)} %iota_compare_fusion.1, f32[2,31]{0,1:T(8,128)S(1)} %copy.4), kind=kLoop, calls=%fused_computation.2 | loop fusion | flops 854000 | bytes 273248 | tf_op jit(solution)/shard_map/reduce_sum | solution.py:19
  6.8 0.7 pad_maximum_fusion.xf
  7.5 0.3 iota_compare_fusion
  7.8 1.0 select_reduce_fusion
  9.0 0.7 maximum_maximum_fusion.1.za
  9.6 0.7 maximum_maximum_fusion.zf
  10.3 124.9 %shard_map.37 = f32[40,64,128]{2,1,0:T(8,128)} custom-call(bf16[2,40,64,128]{3,2,1,0:T(8,128)(2,1)} %data_ref.1, f32[40,64,128]{2,1,0:T(8,128)} %est_ref.1, bf16[2,80,224]{2,1,0:T(8,128)(2,1)} %pad_maximum_fusion.xf, bf16[2,64,128]{2,1,0:T(8,128)(2,1)} %pad_maximum_fusion.3.yf, bf16[256,256]{1,0:T(8,128)(2,1)} %maximum_maximum_fusion.zf, ...), custom_call_target="tpu_custom_call" | custom-call | tf_op jit(solution)/shard_map/pallas_call | solution.py:363
  135.2 2.5 %copy.7 = f32[40,64,128]{2,1,0:T(8,128)} copy(f32[40,64,128]{2,1,0:T(8,128)} %shard_map.37) | data formatting | bytes 2621440
  (13 shorter events, 0.2 us)

commit v2 on v1

--- a/solution.py
+++ b/solution.py
@@ -6,6 +6,7 @@
 from jax.sharding import PartitionSpec as P
 
 ITERS = 3
+TAPS = 31
 GROUP = 4
 ST = 65
 F32 = jnp.float32
@@ -13,46 +14,30 @@
 MESH = pl.DeviceIdType.MESH
 
 
-def band(taps, n_rows, n_cols, shift):
-    offset = jnp.arange(n_cols)[None, :] - jnp.arange(n_rows)[:, None] + shift
-    hit = offset[:, :, None] == jnp.arange(taps.shape[-1])[None, None, :]
-    return jnp.sum(jnp.where(hit[None], taps[:, None, None, :], 0.0), axis=3)
-
-
 def split(w):
     hi = w.astype(BF16)
     return hi, (w - hi.astype(F32)).astype(BF16)
 
 
-def split_weights(w):
-    hi = lax.reduce_precision(w, 8, 7)
-    return hi.astype(BF16), (w - hi).astype(BF16)
-
-
 def dot(a, b):
     return jnp.dot(a, b, preferred_element_type=F32)
 
 
-def make_weights(taps, ny, nz, rows, ext, mid, ext_pad, mid_pad):
-    half = taps.shape[2] // 2
-    flipped = taps[:, :, ::-1]
-    cat = jnp.concatenate
-
-    def along_x(t, n_out, n_in, out_pad, in_pad):
-        w = band(t, n_out, n_in, 0)
-        w = jnp.pad(w, ((0, 0), (0, out_pad - n_out), (0, in_pad - n_in)))
-        return cat(split_weights(w), axis=2)
-
-    xf = along_x(taps[:, 0], mid, ext, mid_pad, ext_pad)
-    xa = along_x(flipped[:, 0], rows, mid, rows, mid_pad)
-    yf = cat(split_weights(band(taps[:, 1], ny, ny, half)), axis=2)
-    hi, lo = split_weights(band(flipped[:, 1], ny, ny, half))
-    ya = cat([hi, lo, hi], axis=2)
-    hi, lo = split_weights(band(flipped[:, 2], nz, nz, half))
-    zf = cat([cat([hi[0], hi[1]], axis=1), cat([lo[0], lo[1]], axis=1)], axis=0)
-    hi, lo = split_weights(band(taps[:, 2], nz, nz, half))
-    za = cat([cat([hi[0], lo[0]], axis=1), cat([hi[1], lo[1]], axis=1)], axis=0)
-    return xf, yf, zf, xa, ya, za
+def band(tap, n_rows, n_cols, blocks, shift, low):
+    col = lax.broadcasted_iota(jnp.int32, (n_rows, blocks * n_cols), 1)
+    row = lax.broadcasted_iota(jnp.int32, (n_rows, blocks * n_cols), 0)
+    is_low = jnp.zeros(col.shape, jnp.bool_)
+    at = col
+    for i in range(1, blocks):
+        at = jnp.where(col >= i * n_cols, col - i * n_cols, at)
+    for i in low:
+        is_low = (col >= i * n_cols) & (col < (i + 1) * n_cols)
+    offset = at - row + shift
+    w = jnp.zeros(col.shape, F32)
+    for k in range(TAPS):
+        w = jnp.where(offset == k, tap(k), w)
+    hi = w.astype(BF16).astype(F32)
+    return jnp.where(is_low, w - hi, hi).astype(BF16)
 
 
 def shards(data, estimate, psf_taps):
@@ -66,9 +51,8 @@
     ext_pad = -(-ext // 16) * 16
     mid_pad = -(-mid // 16) * 16
     ch = rows // 4
-    weights = make_weights(psf_taps, ny, nz, rows, ext, mid, ext_pad, mid_pad)
-
-    def kernel(data_ref, est_ref, xf, yf, zf, xa, ya, za, out_ref,
+
+    def kernel(data_ref, est_ref, taps, out_ref, xf, yf, zf, xa, ya, za,
                extb, zb, xb, rb, ab, yb, dx, em, ps, pr, po, hs, hr, fin,
                lsem, dsem_s, dsem_r, hsem_s, hsem_r, fsem_s, fsem_r,
                psem_s, psem_r, ysem_s, ysem_r, osem_s, osem_r):
@@ -135,7 +119,7 @@
                 at = (ext - wide) - (ext - wide - 2 * ch) * d
                 take = ((d == 0) & has_right) | ((d == 1) & has_left)
             return remote(extb.at[k, pl.ds(at, ch)], extb.at[k, pl.ds(at, ch)],
-                          fsem_s.at[k, which], fsem_r.at[k, which], t, other), take
+                          fsem_s.at[k, which], fsem_r.at[k, which], t, other), at, take
 
         def start_halo(k, which):
             give = piece(k, which)[3]
@@ -144,20 +128,29 @@
             def _():
                 halo(k, which).start()
 
-        def finish_halo(k):
-            for which in (0, 1, 2):
-                take = piece(k, which)[4]
+        def finish_halo(k, between):
+            def arrive(which):
+                at, take = piece(k, which)[1], piece(k, which)[4]
 
                 @pl.when(take)
                 def _():
                     halo(k, which).wait_recv()
                     forward(k, which).start()
+
+            arrive(0)
+            arrive(1)
+            between()
+            blur_z(k, piece(k, 0)[1])
+            blur_z(k, piece(k, 1)[1])
+            arrive(2)
+            blur_z(k, piece(k, 2)[1])
             for which in (0, 1, 2):
-                cp, take = forwarded(k, which)
+                cp, at, take = forwarded(k, which)
 
                 @pl.when(take)
                 def _():
                     cp.wait_recv()
+                blur_z(k, at)
 
         def drain_halo(k):
             for which in (0, 1, 2):
@@ -207,17 +200,28 @@
             zb[i, pl.ds(ext * ST, (ext_pad - ext) * ST), :] = jnp.zeros(((ext_pad - ext) * ST, nz), F32)
             rb[i, pl.ds(mid * ST, (mid_pad - mid) * ST), :] = jnp.zeros(((mid_pad - mid) * ST, nz), F32)
 
-        def blur_z(k):
-            step = ext // 10
-
-            def body(j, _):
-                lhs = extb[k, pl.ds(j * step, step)].reshape(step * ny, nz)
-                o = dot(jnp.concatenate([lhs, lhs], axis=1), zf[...])
-                for q in range(step):
-                    for i in range(views):
-                        zb[i, pl.ds((j * step + q) * ST, ny), :] = o[q * ny:(q + 1) * ny, i * nz:(i + 1) * nz]
-                return 0
-            lax.fori_loop(0, 10, body, 0)
+        for i in range(views):
+            def forth(d, i=i):
+                return lambda q: taps[i, d, q]
+
+            def back(d, i=i):
+                return lambda q: taps[i, d, TAPS - 1 - q]
+
+            w = band(back(2), nz, nz, 2, half, (1,))
+            zf[pl.ds(0, nz), i * nz:(i + 1) * nz] = w[:, :nz]
+            zf[pl.ds(nz, nz), i * nz:(i + 1) * nz] = w[:, nz:]
+            xf[i] = band(forth(0), mid_pad, ext_pad, 2, 0, (1,))
+            yf[i] = band(forth(1), ny, ny, 2, half, (1,))
+            xa[i] = band(back(0), rows, mid_pad, 2, 0, (1,))
+            ya[i] = band(back(1), ny, ny, 3, half, (1,))
+            za[pl.ds(i * nz, nz), :] = band(forth(2), nz, nz, 2, half, (1,))
+
+        def blur_z(k, row):
+            lhs = extb[k, pl.ds(row, ch)].reshape(ch * ny, nz)
+            o = dot(jnp.concatenate([lhs, lhs], axis=1), zf[...])
+            for q in range(ch):
+                for i in range(views):
+                    zb[i, pl.ds((row + q) * ST, ny), :] = o[q * ny:(q + 1) * ny, i * nz:(i + 1) * nz]
 
         def conv_x(src, dst, w, n_in, n_out):
             def body(j, _):
@@ -281,11 +285,12 @@
             row = (ch + ch * (1 - c), 3 * ch * (1 - c))[p]
             return remote(own(k + 1, row), own(k + 1, row), osem_s.at[k, p], osem_r.at[k, p], t, other)
 
-        finish_halo(0)
+        for p in range(4):
+            blur_z(0, wide + ch * p)
+        finish_halo(0, lambda: None)
         cp_dat.wait()
 
         def iteration(k, _):
-            blur_z(k)
             conv_x(zb, xb, xf, ext_pad, mid_pad)
 
             @pl.when((k == 0) & has_left)
@@ -318,12 +323,15 @@
                     for which in ((0, 1), (2,))[p]:
                         start_halo(k + 1, which)
                     share(k, p).start()
+                    blur_z(k + 1, wide + ours[p])
 
             @pl.when(k < ITERS - 1)
             def _():
-                finish_halo(k + 1)
-                for p in (0, 1):
-                    shared(k, p).wait_recv()
+                def between():
+                    for p in (0, 1):
+                        shared(k, p).wait_recv()
+                        blur_z(k + 1, wide + theirs[p])
+                finish_halo(k + 1, between)
             return 0
 
         lax.fori_loop(0, ITERS, iteration, 0)
@@ -363,9 +371,15 @@
     return pl.pallas_call(
         kernel,
         out_shape=jax.ShapeDtypeStruct(estimate.shape, F32),
-        in_specs=[pl.BlockSpec(memory_space=pl.ANY)] * 2 + [pl.BlockSpec(memory_space=vmem)] * 6,
+        in_specs=[pl.BlockSpec(memory_space=pl.ANY)] * 2 + [pl.BlockSpec(memory_space=pltpu.SMEM)],
         out_specs=pl.BlockSpec(memory_space=pl.ANY),
         scratch_shapes=[
+            vmem((views, mid_pad, 2 * ext_pad), BF16),
+            vmem((views, ny, 2 * ny), BF16),
+            vmem((2 * nz, 2 * nz), BF16),
+            vmem((views, rows, 2 * mid_pad), BF16),
+            vmem((views, ny, 3 * ny), BF16),
+            vmem((2 * nz, 2 * nz), BF16),
             vmem((ITERS, ext, ny, nz), BF16),
             vmem((views, ext_pad * ST, nz), F32),
             vmem((views, mid_pad * ST, nz), F32),
@@ -387,7 +401,7 @@
         ],
         compiler_params=pltpu.CompilerParams(
             collective_id=0, has_side_effects=True, vmem_limit_bytes=60 * 1024 * 1024),
-    )(data, estimate, *weights)
+    )(data, estimate, psf_taps)
 
 
 def solution(mesh):

time: 138 us -> 127 us (0.920); the launches traced: 138 us -> 124 us
  other arithmetic: 9.06 us -> 0 us
  Pallas kernels: 125 us -> 121 us
    pallas_call x1, Pallas kernels: 125 us -> 121 us  [shards(): pl.pallas_call(kernel, out_shape=jax.ShapeDtypeStruct(estimate.shape, F32...]
    concatenate x6 -> x0, other arithmetic: 4.17 us -> none  [the longest x2 1.43 us: along_x(): return cat(split_weights(w), axis=2)]
    reduce_sum x4 -> x0, other arithmetic: 4.07 us -> none  [band(): return jnp.sum(jnp.where(hit[None], taps[:, None, None, :], 0.0), axis=3)]
    unnamed x1 -> x2, local copies, waits for them, and re-layouts: 2.52 us -> 3.8 us
where the time goes in v2:
time: 127 us; the launch traced here: 124 us
  Pallas kernels  121 us (95%)
  local copies, waits for them, and re-layouts  3.8 us (3%)
    pallas_call x1, Pallas kernels, shards(): pl.pallas_call(kernel, out_shape=jax.ShapeDtypeStruct(estimate.shape, F32...  121 us
    unnamed x2, local copies, waits for them, and re-layouts  3.8 us

profile of v2, /device:TPU:225, one launch (start us, length us, event | category | flops | bytes accessed | tf_op | source)
XLA Modules:
  0.0 124.4 jit_solution(9848057609273396657)
XLA Ops:
  0.0 1.3 %copy.4.taps = f32[2,3,31]{2,1,0:T(4,128)} copy(f32[2,3,31]{2,0,1:T(2,128)} %param.5) | data formatting | bytes 1488 | tf_op args[2]
  1.3 120.6 %shard_map.37 = f32[40,64,128]{2,1,0:T(8,128)} custom-call(bf16[2,40,64,128]{3,2,1,0:T(8,128)(2,1)} %data_ref.1, f32[40,64,128]{2,1,0:T(8,128)} %est_ref.1, f32[2,3,31]{2,1,0:T(4,128)} %copy.4.taps), custom_call_target="tpu_custom_call" | custom-call | tf_op jit(solution)/shard_map/pallas_call | solution.py:371
  121.9 2.5 %copy.6 = f32[40,64,128]{2,1,0:T(8,128)} copy(f32[40,64,128]{2,1,0:T(8,128)} %shard_map.37) | data formatting | bytes 2621440

commit v3 on v2

--- a/solution.py
+++ b/solution.py
@@ -17,6 +17,20 @@
 def split(w):
     hi = w.astype(BF16)
     return hi, (w - hi.astype(F32)).astype(BF16)
+
+
+TOP = 2.0 ** 7.5
+
+
+def encode(h, m):
+    w = jnp.maximum(h * (TOP / m), 1.0 / TOP)
+    for _ in range(4):
+        w = w * w
+    return w.astype(BF16)
+
+
+def decode(code, m):
+    return jnp.exp(jnp.log(code.astype(F32)) * 0.0625) * (m * (1.0 / TOP))
 
 
 def dot(a, b):
@@ -53,9 +67,9 @@
     ch = rows // 4
 
     def kernel(data_ref, est_ref, taps, out_ref, xf, yf, zf, xa, ya, za,
-               extb, zb, xb, rb, ab, yb, dx, em, ps, pr, po, hs, hr, fin,
+               extb, zb, xb, rb, ab, yb, dx, em, ps, pr, po, hs, hr, ms, mr, fin,
                lsem, dsem_s, dsem_r, hsem_s, hsem_r, fsem_s, fsem_r,
-               psem_s, psem_r, ysem_s, ysem_r, osem_s, osem_r):
+               psem_s, psem_r, ysem_s, ysem_r, osem_s, osem_r, msem_s, msem_r):
         t = lax.axis_index("tile")
         v = lax.axis_index("view")
         c = lax.rem(v, 2)
@@ -277,6 +291,12 @@
         def over(k, p):
             return remote(hs.at[k, p], hr.at[k, p], ysem_s.at[k, p], ysem_r.at[k, p], t, across)
 
+        def over_scale(k, p):
+            return remote(ms.at[k, p], mr.at[k, p], msem_s.at[k, p], msem_r.at[k, p], t, across)
+
+        def scale_of(ref, k, p):
+            return ref[k, p].astype(F32)[:1].reshape(1, 1, nz)
+
         def share(k, p):
             row = (inner, outer)[p]
             return remote(own(k + 1, row), own(k + 1, row), osem_s.at[k, p], osem_r.at[k, p], t, other)
@@ -310,12 +330,17 @@
                 partner(k, p).start()
                 po[p] = adjoint_rows(ours[p])
                 partner(k, p).wait_recv()
-                hs[k, p] = po[p] + pr[k, p]
+                both = po[p] + pr[k, p]
+                ms[k, p] = jnp.full((16, nz), jnp.max(both) * 1.01, F32).astype(BF16)
+                hs[k, p] = encode(both, scale_of(ms, k, p))
+                over_scale(k, p).start()
                 over(k, p).start()
             for p in (0, 1):
+                over_scale(k, p).wait_recv()
                 over(k, p).wait_recv()
+                total = decode(hs[k, p], scale_of(ms, k, p)) + decode(hr[k, p], scale_of(mr, k, p))
                 rows_here = pl.ds(ours[p], ch)
-                em[rows_here] = em[rows_here] * (hs[k, p] + hr[k, p]) / total_views
+                em[rows_here] = em[rows_here] * total / total_views
 
                 @pl.when(k < ITERS - 1)
                 def _():
@@ -362,6 +387,7 @@
             for p in (0, 1):
                 partner(k, p).wait_send()
                 over(k, p).wait_send()
+                over_scale(k, p).wait_send()
                 if k < ITERS - 1:
                     share(k, p).wait_send()
 
@@ -391,13 +417,15 @@
             vmem((ITERS, 2) + block, F32),
             vmem((ITERS, 2) + block, F32),
             vmem((2,) + block, F32),
-            vmem((ITERS, 2) + block, F32),
-            vmem((ITERS, 2) + block, F32),
+            vmem((ITERS, 2) + block, BF16),
+            vmem((ITERS, 2) + block, BF16),
+            vmem((ITERS, 2, 16, nz), BF16),
+            vmem((ITERS, 2, 16, nz), BF16),
             vmem((2,) + block, F32),
             dma((4,)), dma((2,)), dma((2,)),
             dma((ITERS, 3)), dma((ITERS, 3)), dma((ITERS, 3)), dma((ITERS, 3)),
             dma((ITERS, 2)), dma((ITERS, 2)), dma((ITERS, 2)), dma((ITERS, 2)),
-            dma((ITERS, 2)), dma((ITERS, 2)),
+            dma((ITERS, 2)), dma((ITERS, 2)), dma((ITERS, 2)), dma((ITERS, 2)),
         ],
         compiler_params=pltpu.CompilerParams(
             collective_id=0, has_side_effects=True, vmem_limit_bytes=60 * 1024 * 1024),

time: 127 us -> 108 us (0.85); the launches traced: 124 us -> 107 us
  Pallas kernels: 121 us -> 103 us
    pallas_call x1, Pallas kernels: 121 us -> 103 us  [shards(): pl.pallas_call(kernel, out_shape=jax.ShapeDtypeStruct(estimate.shape, F32...]
where the time goes in v3:
time: 108 us; the launch traced here: 107 us
  Pallas kernels  103 us (95%)
  local copies, waits for them, and re-layouts  3.8 us (4%)
    pallas_call x1, Pallas kernels, shards(): pl.pallas_call(kernel, out_shape=jax.ShapeDtypeStruct(estimate.shape, F32...  103 us
    unnamed x2, local copies, waits for them, and re-layouts  3.8 us

profile of v3, /device:TPU:225, one launch (start us, length us, event | category | flops | bytes accessed | tf_op | source)
XLA Modules:
  0.0 107.1 jit_solution(16595034931800022575)
XLA Ops:
  0.0 1.3 %copy.4.taps = f32[2,3,31]{2,1,0:T(4,128)} copy(f32[2,3,31]{2,0,1:T(2,128)} %param.5) | data formatting | bytes 1488 | tf_op args[2]
  1.3 103.3 %shard_map.37 = f32[40,64,128]{2,1,0:T(8,128)} custom-call(bf16[2,40,64,128]{3,2,1,0:T(8,128)(2,1)} %data_ref.1, f32[40,64,128]{2,1,0:T(8,128)} %est_ref.1, f32[2,3,31]{2,1,0:T(4,128)} %copy.4.taps), custom_call_target="tpu_custom_call" | custom-call | tf_op jit(solution)/shard_map/pallas_call | solution.py:397
  104.5 2.5 %copy.6 = f32[40,64,128]{2,1,0:T(8,128)} copy(f32[40,64,128]{2,1,0:T(8,128)} %shard_map.37) | data formatting | bytes 2621440
